TPU v7x, 32 devices: a whole 2x2x4 slice. The times are simulated.
32 devices in a mesh: row: 8 (over z, y), col: 4 (over x, core).
Axes of the slice: x: 2, y: 2, z: 4, core: 2. Of those that a mesh axis runs over, the one named last changes fastest.
Arguments:
- anc_inverse: float32 [20480, 20480], P('row', 'col'), may hold values from -6 to 6
- l_store: float32 [4, 20480, 256], P('col', 'row'), may hold values from -0.0546875 to 0.0546875
- diag_inv: float32 [4, 256, 256], P('col'), may hold values from -6 to 6
- block_lists: int32 [4, 96], replicated, may hold values from 0 to 159, as said below
- block_counts: int32 [4], replicated, may hold values from 48 to 96, as said below
- sibling_columns: int32 [4], replicated, may hold values from 0 to 3, as said below
Outputs:
- upper_out: float32 [4, 256, 20480], P(None, 'row', 'col')
- lower_out: float32 [4, 20480, 256], P('col', 'row')
- diag_out: float32 [4, 256, 256], P('col')
Inputs may be any that keep to these rules, and one draw needn't show every extreme that they name: `block_lists`: in each sibling's row the entries are distinct block indices; entries at positions from block_counts onward are ignored. `block_counts`: some sibling uses all 96 entries. `sibling_columns`: distinct columns for distinct siblings.
All inputs are finite; a program needn't handle non-finite values.
Results may differ from a plain program's by a relative error of at most 0.00011.
Values sent between devices are 32-bit elements; how exact they have to be, the bound alone decides.
A program may use at most 128 MiB of HBM per device.

v0:
```python
import functools

import jax
import jax.numpy as jnp
from jax import lax
from jax.experimental import pallas as pl
from jax.experimental.pallas import tpu as pltpu
from jax.sharding import PartitionSpec as P

BLK = 128
MESH = pl.DeviceIdType.MESH


def listed_table(block_lists, block_counts, block_total):
    block_ids = jnp.arange(block_total, dtype=jnp.int32)
    valid_entry = jnp.arange(block_lists.shape[1], dtype=jnp.int32)[None, :] < block_counts[:, None]
    entry_hits = (block_lists[:, :, None] == block_ids[None, None, :]) & valid_entry[:, :, None]
    return jnp.any(entry_hits, axis=1)


def product_kernel(siblings, tile_blocks, col_blocks, row_blocks,
                   slot_ref, rows_ref, count_ref, column_ref,
                   a_ref, panels_ref, out_ref, a_high, a_low, p_high, p_low, acc):
    stripe = pl.program_id(0)
    width = out_ref.shape[0]

    @pl.when(stripe == 0)
    def _():
        for sibling in range(siblings):
            column = column_ref[sibling]

            @pl.loop(0, row_blocks)
            def _(block):
                lanes = pl.ds(pl.multiple_of(block * BLK, BLK), BLK)
                value = panels_ref[pl.ds(pl.multiple_of(column * width, width), width), lanes]
                high = value.astype(jnp.bfloat16)
                p_high[sibling, block] = high
                p_low[sibling, block] = (value - high.astype(jnp.float32)).astype(jnp.bfloat16)

            p_high[sibling, row_blocks] = jnp.zeros(p_high.shape[2:], jnp.bfloat16)
            p_low[sibling, row_blocks] = jnp.zeros(p_low.shape[2:], jnp.bfloat16)

    @pl.loop(0, row_blocks)
    def _(block):
        rows = pl.ds(pl.multiple_of(block * BLK, BLK), BLK)
        value = a_ref[rows, :]
        high = value.astype(jnp.bfloat16)
        a_high[block] = high
        a_low[block] = (value - high.astype(jnp.float32)).astype(jnp.bfloat16)

    for sibling in range(siblings):
        acc[...] = jnp.zeros_like(acc)
        base = sibling * (row_blocks + 1)

        @pl.loop(0, (count_ref[sibling] + 1) // 2)
        def _(pair):
            first = rows_ref[base + 2 * pair]
            second = rows_ref[base + 2 * pair + 1]
            second_a = jnp.minimum(second, row_blocks - 1)
            ph = [p_high[sibling, first], p_high[sibling, second]]
            plo = [p_low[sibling, first], p_low[sibling, second]]
            ah = [a_high[first], a_high[second_a]]
            al = [a_low[first], a_low[second_a]]
            left = jnp.concatenate(ph + ph + plo, axis=1)
            right = jnp.concatenate(ah + al + ah, axis=0)
            acc[...] += jnp.dot(left, right, preferred_element_type=jnp.float32)

        for block in range(tile_blocks):
            slot = slot_ref[sibling * col_blocks + stripe * tile_blocks + block]

            @pl.when(slot >= 0)
            def _():
                out_ref[:, pl.ds(pl.multiple_of(slot * BLK, BLK), BLK)] = (
                    -acc[:, block * BLK:(block + 1) * BLK]
                )


def product(slot, rows, counts, columns, anc, panels, width, cap):
    siblings = counts.shape[0]
    depth, cells = anc.shape
    row_blocks, col_blocks = depth // BLK, cells // BLK
    tile_blocks = next(n for n in (4, 2, 1) if col_blocks % n == 0)
    tile = tile_blocks * BLK
    return pl.pallas_call(
        functools.partial(product_kernel, siblings, tile_blocks, col_blocks, row_blocks),
        out_shape=jax.ShapeDtypeStruct((width, cap * BLK), jnp.float32),
        grid_spec=pltpu.PrefetchScalarGridSpec(
            num_scalar_prefetch=4,
            grid=(col_blocks // tile_blocks,),
            in_specs=[
                pl.BlockSpec((depth, tile), lambda i, *_: (0, i)),
                pl.BlockSpec(panels.shape, lambda i, *_: (0, 0), pipeline_mode=pl.Buffered(1)),
            ],
            out_specs=pl.BlockSpec((width, cap * BLK), lambda i, *_: (0, 0), pipeline_mode=pl.Buffered(1)),
            scratch_shapes=[
                pltpu.VMEM((row_blocks, BLK, tile), jnp.bfloat16),
                pltpu.VMEM((row_blocks, BLK, tile), jnp.bfloat16),
                pltpu.VMEM((siblings, row_blocks + 1, width, BLK), jnp.bfloat16),
                pltpu.VMEM((siblings, row_blocks + 1, width, BLK), jnp.bfloat16),
                pltpu.VMEM((width, tile), jnp.float32),
            ],
        ),
        compiler_params=pltpu.CompilerParams(
            dimension_semantics=("arbitrary",), vmem_limit_bytes=63 * 1024 * 1000
        ),
    )(slot, rows, counts, columns, anc, panels)


def flip_kernel(value_ref, out_ref):
    out_ref[...] = value_ref[...].T


def flipped(value):
    depth, width = value.shape
    step = next(n for n in (512, 256, 128) if depth % n == 0)
    return pl.pallas_call(
        flip_kernel,
        out_shape=jax.ShapeDtypeStruct((width, depth), value.dtype),
        grid=(depth // step,),
        in_specs=[pl.BlockSpec((step, width), lambda i: (i, 0))],
        out_specs=pl.BlockSpec((width, step), lambda i: (0, i)),
    )(value)


def expand_kernel(siblings, col_count, col_blocks, slot_ref, owner_ref, compact_ref, upper_ref, slots_ref):
    @pl.loop(0, col_blocks)
    def _(block):
        lanes = pl.ds(pl.multiple_of(block * BLK, BLK), BLK)
        for sibling in range(siblings):
            slot = slot_ref[sibling * col_blocks + block]
            at = pl.ds(pl.multiple_of(jnp.maximum(slot, 0) * BLK, BLK), BLK)
            value = compact_ref[:, at]
            upper_ref[sibling, :, lanes] = jnp.where(slot >= 0, value, jnp.zeros_like(value))

    for column in range(col_count):
        sibling = owner_ref[column]
        value = upper_ref[jnp.maximum(sibling, 0)]
        slots_ref[column] = jnp.where(sibling >= 0, value, jnp.zeros_like(value))


def expand(slot, owner, compact, siblings, col_blocks):
    col_count = owner.shape[0]
    rows = compact.shape[0]
    return pl.pallas_call(
        functools.partial(expand_kernel, siblings, col_count, col_blocks),
        out_shape=(
            jax.ShapeDtypeStruct((siblings, rows, col_blocks * BLK), jnp.float32),
            jax.ShapeDtypeStruct((col_count, rows, col_blocks * BLK), jnp.float32),
        ),
        in_specs=[pl.BlockSpec(memory_space=pltpu.SMEM)] * 2 + [pl.BlockSpec(memory_space=pltpu.VMEM)],
        out_specs=(pl.BlockSpec(memory_space=pltpu.VMEM),) * 2,
    )(slot, owner, compact)


def reduce_kernel(line, flat_first, chunks,
                  partial_ref, out_ref,
                  pair_buf, up_buf, down_buf, flat_up, flat_down, flat_sum, flat_pair,
                  pair_send, pair_recv, up_send, up_recv, down_send, down_recv, flat_send, flat_recv):
    r, c = lax.axis_index("row"), lax.axis_index("col")
    z, y = r // 2, lax.rem(r, 2)
    other = 1 - y
    width = out_ref.shape[1] // chunks
    last, lag = line - 1, 2
    late = chunks - flat_first

    def lanes(chunk):
        return pl.ds(pl.multiple_of(chunk * width, width), width)

    barrier = pltpu.get_barrier_semaphore()
    pl.semaphore_signal(barrier, inc=1, device_id=(z * 2 + other, c), device_id_type=MESH)

    @pl.when(z > 0)
    def _():
        pl.semaphore_signal(barrier, inc=1, device_id=(r - 2, c), device_id_type=MESH)

    @pl.when(z < last)
    def _():
        pl.semaphore_signal(barrier, inc=1, device_id=(r + 2, c), device_id_type=MESH)

    pl.semaphore_wait(barrier, 1 + (z > 0).astype(jnp.int32) + (z < last).astype(jnp.int32))

    def pair_copy(k):
        return pltpu.make_async_remote_copy(
            src_ref=partial_ref.at[:, other, :, lanes(k + flat_first)],
            dst_ref=pair_buf.at[k],
            send_sem=pair_send.at[k],
            recv_sem=pair_recv.at[k],
            device_id=(z * 2 + other, c),
            device_id_type=MESH,
        )

    def flat_copy(k):
        return pltpu.make_async_remote_copy(
            src_ref=flat_sum.at[k, other],
            dst_ref=flat_pair.at[k],
            send_sem=flat_send.at[k],
            recv_sem=flat_recv.at[k],
            device_id=(z * 2 + other, c),
            device_id_type=MESH,
        )

    def up_copy(buf, k, slot, at):
        return pltpu.make_async_remote_copy(
            src_ref=buf.at[k, pl.ds(at, last - at)],
            dst_ref=buf.at[k, pl.ds(at, last - at)],
            send_sem=up_send.at[slot],
            recv_sem=up_recv.at[slot],
            device_id=(r + 2, c),
            device_id_type=MESH,
        )

    def down_copy(buf, k, slot, at):
        return pltpu.make_async_remote_copy(
            src_ref=buf.at[k, pl.ds(0, at)],
            dst_ref=buf.at[k, pl.ds(0, at)],
            send_sem=down_send.at[slot],
            recv_sem=down_recv.at[slot],
            device_id=(r - 2, c),
            device_id_type=MESH,
        )

    def flat(k):
        def own(place):
            return partial_ref[place, :, :, lanes(k)]

        def finish(value):
            flat_sum[k] = value
            flat_copy(k).start()

        return flat_up, flat_down, k, own, finish

    def paired(k):
        k = k - flat_first

        def own(place):
            return pair_buf[k, place]

        def finish(value):
            out_ref[:, lanes(k + flat_first)] = value

        return up_buf, down_buf, k, own, finish

    def total(at, up, down, k, own, finish):
        value = own(at)
        if at > 0:
            value = value + up[k, at - 1]
        if at < last:
            value = value + down[k, at]
        finish(value)

    def pass_up(at, slot, up, down, k, own, finish):
        if at > 0:
            up_copy(up, k, slot, at - 1).wait_recv()
        for place in range(at + 1, line):
            if at > 0:
                up[k, place - 1] = up[k, place - 1] + own(place)
            else:
                up[k, place - 1] = own(place)
        if at < last:
            up_copy(up, k, slot, at).start()
        if 2 * at > last:
            total(at, up, down, k, own, finish)

    def pass_down(at, slot, up, down, k, own, finish):
        if at < last:
            down_copy(down, k, slot, at + 1).wait_recv()
        for place in range(at):
            if at < last:
                down[k, place] = down[k, place] + own(place)
            else:
                down[k, place] = own(place)
        if at > 0:
            down_copy(down, k, slot, at).start()
        if 2 * at <= last:
            total(at, up, down, k, own, finish)

    def either(step, at, slot):
        @pl.when((slot >= 0) & (slot < flat_first))
        def _():
            step(at, slot, *flat(slot))

        @pl.when((slot >= flat_first) & (slot < chunks))
        def _():
            step(at, slot, *paired(slot))

    @pl.loop(0, late)
    def _(k):
        pair_copy(k).start()

    @pl.loop(0, chunks + lag * last)
    def _(i):
        @pl.when((i >= flat_first) & (i < chunks))
        def _():
            k = i - flat_first
            pair_copy(k).wait_recv()
            for place in range(line):
                pair_buf[k, place] = pair_buf[k, place] + partial_ref[place, y, :, lanes(i)]

        for at in range(line):
            @pl.when(z == at)
            def _():
                either(pass_up, at, i - lag * at)
                either(pass_down, at, i - lag * (last - at))

    @pl.loop(0, flat_first)
    def _(k):
        flat_copy(k).wait_recv()
        out_ref[:, lanes(k)] = flat_sum[k, y] + flat_pair[k]

    @pl.loop(0, late)
    def _(k):
        pair_copy(k).wait_send()

    @pl.loop(0, flat_first)
    def _(k):
        flat_copy(k).wait_send()

    for at in range(line):
        @pl.when(z == at)
        def _():
            for buf, start, stop, shift in ((flat_up, 0, flat_first, 0), (up_buf, 0, late, flat_first)):
                if at < last:
                    @pl.loop(start, stop)
                    def _(k):
                        up_copy(buf, k, k + shift, at).wait_send()
            for buf, start, stop, shift in ((flat_down, 0, flat_first, 0), (down_buf, 0, late, flat_first)):
                if at > 0:
                    @pl.loop(start, stop)
                    def _(k):
                        down_copy(buf, k, k + shift, at).wait_send()


def reduce_rows(value, row_count, chunks, collective):
    width, columns = value.shape
    line, slice_rows = row_count // 2, width // row_count
    lanes = columns // chunks
    flat_first = (chunks + 3) // 6
    late = chunks - flat_first
    vmem = pl.BlockSpec(memory_space=pltpu.VMEM)
    dma = pltpu.SemaphoreType.DMA
    return pl.pallas_call(
        functools.partial(reduce_kernel, line, flat_first, chunks),
        out_shape=jax.ShapeDtypeStruct((slice_rows, columns), jnp.float32),
        in_specs=[vmem],
        out_specs=vmem,
        scratch_shapes=[
            pltpu.VMEM((late, line, slice_rows, lanes), jnp.float32),
            pltpu.VMEM((late, line - 1, slice_rows, lanes), jnp.float32),
            pltpu.VMEM((late, line - 1, slice_rows, lanes), jnp.float32),
            pltpu.VMEM((flat_first, line - 1, 2, slice_rows, lanes), jnp.float32),
            pltpu.VMEM((flat_first, line - 1, 2, slice_rows, lanes), jnp.float32),
            pltpu.VMEM((flat_first, 2, slice_rows, lanes), jnp.float32),
            pltpu.VMEM((flat_first, slice_rows, lanes), jnp.float32),
            dma((late,)),
            dma((late,)),
            dma((chunks,)),
            dma((chunks,)),
            dma((chunks,)),
            dma((chunks,)),
            dma((flat_first,)),
            dma((flat_first,)),
        ],
        compiler_params=pltpu.CompilerParams(
            collective_id=collective, has_side_effects=True, vmem_limit_bytes=63 * 1024 * 1000
        ),
    )(value.reshape(line, 2, slice_rows, columns))


def finish_kernel(row_count, col_count,
                  slots_ref, own_ref, base_ref, lower_ref, diag_ref,
                  stage, picked, inner, part, reduced, total,
                  stage_send, stage_recv, send_sem, recv_sem, part_send, part_recv, total_send, total_recv):
    r, c = lax.axis_index("row"), lax.axis_index("col")
    ratio = row_count // col_count
    slice_rows, cells = picked.shape[1], picked.shape[2]

    barrier = pltpu.get_barrier_semaphore()
    for peer in range(row_count):
        @pl.when(peer != r)
        def _():
            pl.semaphore_signal(barrier, inc=1, device_id=(peer, c), device_id_type=MESH)
    for peer in range(col_count):
        @pl.when(peer != c)
        def _():
            pl.semaphore_signal(barrier, inc=1, device_id=(r, peer), device_id_type=MESH)
    pl.semaphore_wait(barrier, row_count + col_count - 2)

    def near(offset):
        pair = lax.rem(c // 2 + offset // 2, col_count // 2)
        return pair * 2 + lax.rem(lax.rem(c, 2) + offset % 2, 2)

    def column_copy(target):
        return pltpu.make_async_remote_copy(
            src_ref=slots_ref.at[target],
            dst_ref=stage.at[c],
            send_sem=stage_send.at[target],
            recv_sem=stage_recv.at[c],
            device_id=(r, target),
            device_id_type=MESH,
        )

    def column_arrived(source):
        return pltpu.make_async_remote_copy(
            src_ref=slots_ref.at[source],
            dst_ref=stage.at[source],
            send_sem=stage_send.at[source],
            recv_sem=stage_recv.at[source],
            device_id=(r, source),
            device_id_type=MESH,
        )

    def row_copy(held, source, k):
        target = source * ratio + k
        return pltpu.make_async_remote_copy(
            src_ref=held.at[source, :, pl.ds(k * cells, cells)],
            dst_ref=picked.at[r],
            send_sem=send_sem.at[target],
            recv_sem=recv_sem.at[r],
            device_id=(target, c),
            device_id_type=MESH,
        )

    def row_local(held, source, k):
        return pltpu.make_async_copy(
            held.at[source, :, pl.ds(k * cells, cells)], picked.at[r], recv_sem.at[r]
        )

    def row_arrived(source):
        return pltpu.make_async_remote_copy(
            src_ref=picked.at[source],
            dst_ref=picked.at[source],
            send_sem=send_sem.at[source],
            recv_sem=recv_sem.at[source],
            device_id=(source, c),
            device_id_type=MESH,
        )

    for offset in range(2, col_count):
        column_copy(near(offset)).start()
    column_copy(near(1)).start()
    for offset in range(col_count):
        source = near(offset)
        held = stage if offset else slots_ref
        if offset:
            column_arrived(source).wait_recv()
        for k in range(ratio):
            @pl.when(source * ratio + k == r)
            def _():
                row_local(held, source, k).start()

            @pl.when(source * ratio + k != r)
            def _():
                row_copy(held, source, k).start()

    for offset in range(col_count):
        source = near(offset)
        held = stage if offset else slots_ref
        for k in range(ratio):
            @pl.when(source * ratio + k == r)
            def _():
                row_local(held, source, k).wait()
    for source in range(row_count):
        @pl.when(source != r)
        def _():
            row_arrived(source).wait_recv()

    step = 256 if cells % 256 == 0 else BLK
    inner[...] = jnp.zeros_like(inner)

    @pl.loop(0, cells // step)
    def _(i):
        at = pl.ds(pl.multiple_of(i * step, step), step)
        block = picked[:, :, at].reshape(row_count * slice_rows, step)
        inner[...] += jnp.dot(
            block, own_ref[at, :], precision=lax.Precision.HIGHEST, preferred_element_type=jnp.float32
        )

    def part_copy(peer):
        return pltpu.make_async_remote_copy(
            src_ref=inner.at[pl.ds(peer * slice_rows, slice_rows), :],
            dst_ref=part.at[r],
            send_sem=part_send.at[peer],
            recv_sem=part_recv.at[r],
            device_id=(peer, c),
            device_id_type=MESH,
        )

    def part_arrived(peer):
        return pltpu.make_async_remote_copy(
            src_ref=inner.at[pl.ds(0, slice_rows), :],
            dst_ref=part.at[peer],
            send_sem=part_send.at[peer],
            recv_sem=part_recv.at[peer],
            device_id=(peer, c),
            device_id_type=MESH,
        )

    def total_copy(peer):
        return pltpu.make_async_remote_copy(
            src_ref=reduced,
            dst_ref=total.at[r],
            send_sem=total_send.at[peer],
            recv_sem=total_recv.at[r],
            device_id=(peer, c),
            device_id_type=MESH,
        )

    def total_arrived(peer):
        return pltpu.make_async_remote_copy(
            src_ref=reduced,
            dst_ref=total.at[peer],
            send_sem=total_send.at[peer],
            recv_sem=total_recv.at[peer],
            device_id=(peer, c),
            device_id_type=MESH,
        )

    def peers(action):
        for peer in range(row_count):
            @pl.when(peer != r)
            def _():
                action(peer)

    peers(lambda peer: part_copy(peer).start())
    peers(lambda peer: part_arrived(peer).wait_recv())
    mine = inner[pl.ds(pl.multiple_of(r * slice_rows, slice_rows), slice_rows), :]
    for peer in range(row_count):
        @pl.when(peer == r)
        def _():
            part[peer] = mine
    value = part[0]
    for peer in range(1, row_count):
        value = value + part[peer]
    reduced[...] = value
    peers(lambda peer: total_copy(peer).start())

    @pl.loop(0, cells // step)
    def _(i):
        at = pl.ds(pl.multiple_of(i * step, step), step)
        block = picked[:, :, at].reshape(row_count * slice_rows, step)
        lower_ref[at, :] = block.T

    peers(lambda peer: total_arrived(peer).wait_recv())
    for peer in range(row_count):
        @pl.when(peer == r)
        def _():
            total[peer] = reduced[...]
    diag_ref[...] = base_ref[...] - total[...].reshape(diag_ref.shape)

    for offset in range(col_count):
        source = near(offset)
        held = stage if offset else slots_ref
        if offset:
            column_copy(source).wait_send()
        for k in range(ratio):
            @pl.when(source * ratio + k != r)
            def _():
                row_copy(held, source, k).wait_send()
    peers(lambda peer: part_copy(peer).wait_send())
    peers(lambda peer: total_copy(peer).wait_send())


def finish(slots, own, base, row_count):
    col_count, slice_rows, _ = slots.shape
    cells, width = own.shape
    vmem = pl.BlockSpec(memory_space=pltpu.VMEM)
    dma = pltpu.SemaphoreType.DMA
    return pl.pallas_call(
        functools.partial(finish_kernel, row_count, col_count),
        out_shape=(
            jax.ShapeDtypeStruct((cells, width), jnp.float32),
            jax.ShapeDtypeStruct((width, width), jnp.float32),
        ),
        in_specs=[vmem] * 3,
        out_specs=(vmem, vmem),
        scratch_shapes=[
            pltpu.VMEM(slots.shape, jnp.float32),
            pltpu.VMEM((row_count, slice_rows, cells), jnp.float32),
            pltpu.VMEM((width, width), jnp.float32),
            pltpu.VMEM((row_count, slice_rows, width), jnp.float32),
            pltpu.VMEM((slice_rows, width), jnp.float32),
            pltpu.VMEM((row_count, slice_rows, width), jnp.float32),
            dma((col_count,)),
            dma((col_count,)),
            dma((row_count,)),
            dma((row_count,)),
            dma((row_count,)),
            dma((row_count,)),
            dma((row_count,)),
            dma((row_count,)),
        ],
        compiler_params=pltpu.CompilerParams(collective_id=0, has_side_effects=True),
    )(slots, own, base)


def per_device(anc_inverse, l_store, diag_inv, block_lists, block_counts, sibling_columns):
    siblings = block_lists.shape[0]
    row_count, col_count = lax.axis_size("row"), lax.axis_size("col")
    r, c = lax.axis_index("row"), lax.axis_index("col")
    row_blocks, col_blocks = anc_inverse.shape[0] // BLK, anc_inverse.shape[1] // BLK
    panels = lax.all_gather(flipped(l_store[0]), "col", tiled=True)

    table = listed_table(block_lists, block_counts, row_blocks * row_count)
    row_listed = lax.dynamic_slice_in_dim(table, r * row_blocks, row_blocks, axis=1)
    col_listed = lax.dynamic_slice_in_dim(table, c * col_blocks, col_blocks, axis=1)
    row_ints = row_listed.astype(jnp.int32)
    counts = jnp.sum(row_ints, axis=1)
    place = jnp.cumsum(row_ints, axis=1) - 1
    ids = jnp.arange(row_blocks, dtype=jnp.int32)
    entry = jnp.arange(row_blocks + 1, dtype=jnp.int32)
    hits = row_listed[:, :, None] & (place[:, :, None] == entry[None, None, :])
    rows = jnp.sum(jnp.where(hits, ids[None, :, None], 0), axis=1)
    rows = jnp.where(entry[None, :] < counts[:, None], rows, row_blocks).astype(jnp.int32).reshape(-1)

    flat = col_listed.reshape(-1)
    slot = jnp.where(flat, jnp.cumsum(flat.astype(jnp.int32)) - 1, -1).astype(jnp.int32)
    per_column = jnp.sum(table.reshape(siblings, col_count, col_blocks).astype(jnp.int32), axis=(0, 2))
    needed = jnp.max(per_column)
    slots_all = siblings * col_blocks
    grain = -(-slots_all // 40)
    caps = [grain * n for n in (19, 21, 23, 25, 28, 32, 40)]
    level = jnp.sum((needed > jnp.array(caps[:-1], jnp.int32)).astype(jnp.int32))

    match = sibling_columns[:, None] == jnp.arange(col_count, dtype=jnp.int32)[None, :]
    owner = jnp.max(
        jnp.where(match, jnp.arange(siblings, dtype=jnp.int32)[:, None], -1), axis=0
    ).astype(jnp.int32)
    mine = sibling_columns == c
    own_listed = jnp.any(row_listed & mine[:, None], axis=0)
    own = l_store[0] * jnp.repeat(own_listed.astype(jnp.float32), BLK)[:, None]
    base = jnp.sum(mine.astype(jnp.float32)) * diag_inv[0]

    def branch(place, cap):
        def run(anc, panels):
            partial_value = product(slot, rows, counts, sibling_columns, anc, panels, l_store.shape[2], cap)
            compact = reduce_rows(partial_value, row_count, cap // grain, place + 1)
            return expand(slot, owner, compact, siblings, col_blocks)
        return run

    upper, slots = lax.switch(level, [branch(place, cap) for place, cap in enumerate(caps)], anc_inverse, panels)
    lower, diag = finish(slots, own, base, row_count)
    return upper, lower[None], diag[None]


def solution(mesh):
    return jax.shard_map(
        per_device,
        mesh=mesh,
        in_specs=(P("row", "col"), P("col", "row", None), P("col", None, None), P(), P(), P()),
        out_specs=(P(None, "row", "col"), P("col", "row", None), P("col", None, None)),
        check_vma=False,
    )
```

profile of v0, /device:TPU:0, one launch (start us, length us, event | category | flops | bytes accessed | tf_op | source)
XLA Modules:
  0.0 437.7 jit_solution(7389257471023859446)
XLA Ops:
  7.2 5.2 %shard_map.94 = f32[256,2560]{1,0:T(8,128)} custom-call(f32[2560,256]{1,0:T(8,128)} %bitcast.26), custom_call_target="tpu_custom_call" | custom-call | tf_op jit(solution)/shard_map/pallas_call | solution.py:116
  12.4 0.6 copy-done.5
  13.1 0.2 fusion.1
  13.3 0.7 convert_reduce_fusion.2
  14.1 0.1 copy.10
  14.2 0.2 reduce_window_sum.28
  14.4 0.1 copy.11
  14.5 0.1 convert_reduce_fusion.1
  14.7 0.1 select_reduce_fusion
  15.1 0.3 reduce-window.9
  15.6 0.1 reduce_sum.54
  15.8 0.6 reduce_max.18
  16.4 1.3 fusion.5
  18.3 0.1 slice_reduce_fusion
  18.7 1.4 multiply_bitcast_fusion.base_ref
  20.1 1.9 broadcast_multiply_fusion.own_ref
  22.0 63.5 %all-gather.2.cloned.1.call-done = f32[1024,2560]{1,0:T(8,128)} async-done(((f32[256,2560]{1,0:T(8,128)}), f32[1024,2560]{1,0:T(8,128)}) %all-gather.2.cloned.1.call-update) | async-done | bytes 10485776 | tf_op jit(solution)/shard_map/all_gather | solution.py:601
  85.5 248.4 %conditional.1 = ((f32[4,32,5120]{2,1,0:T(8,128)}, f32[4,32,5120]{2,1,0:T(8,128)S(1)})) conditional(s32[]{:T(128)} %clamp.3, (s32[160]{0:T(256)S(1)}, s32[84]{0:T(128)S(1)}, s32[4]{0:T(128)S(1)}, s32[4]{0:T(128)S(1)}, f32[2560,5120]{1,0:T(8,128)}, /*index=5*/f32[1024,2560]{1,0:T(8,128)}, s32[4]{0:T(128)S(1)}) %tuple.51, ...), branch_computations={%region_11.12_spmd, %region_12.13_spmd, %region_13.14_spmd, %regio... | conditional | bytes 8 | solution.py:640
  85.5 107.0 %branch_2_fun.3 = f32[256,11776]{1,0:T(8,128)} custom-call(s32[160]{0:T(256)S(1)} %get-tuple-element.112.slot_ref, s32[84]{0:T(128)S(1)} %get-tuple-element.114.rows_ref, s32[4]{0:T(128)S(1)} %get-tuple-element.115.count_ref, s32[4]{0:T(128)S(1)} %get-tuple-element.116.column_ref, f32[2560,5120]{1,0:T(8,128)} %get-tuple-element.117.a_ref, ...), custom_call_target="tpu_custom_call" | custom-call | tf_op jit(solution)/shard_map/cond/branch_2_fun/pallas_call | solution.py:84
  192.5 137.4 %branch_2_fun.4.compact_ref = f32[32,11776]{1,0:T(8,128)} custom-call(f32[4,2,32,11776]{3,2,1,0:T(8,128)} %bitcast.23), custom_call_target="tpu_custom_call" | custom-call | tf_op jit(solution)/shard_map/cond/branch_2_fun/pallas_call | solution.py:341
  329.9 3.9 branch_2_fun.5
  333.9 92.8 %shard_map.95 = (f32[2560,256]{1,0:T(8,128)}, f32[256,256]{1,0:T(8,128)}) custom-call(f32[4,32,5120]{2,1,0:T(8,128)S(1)} %get-tuple-element.155.slots_ref, f32[2560,256]{1,0:T(8,128)} %broadcast_multiply_fusion.own_ref, f32[256,256]{1,0:T(8,128)} %multiply_bitcast_fusion.base_ref), custom_call_target="tpu_custom_call" | custom-call | tf_op jit(solution)/shard_map/pallas_call | solution.py:568
  426.7 3.4 copy.28
  430.1 0.7 copy.29
  (33 shorter events, 1.0 us)
Async XLA Ops:
  7.2 78.3 %all-gather.2.cloned.1.call-start = ((), (), s32[]{:S(2)}) async-start(), calls=%async_computation | async-start | bytes 13107200 | tf_op jit(solution)/shard_map/all_gather | solution.py:601
  7.2 11.5 %copy-start.1 = (f32[1,256,256]{2,1,0:T(8,128)S(1)}, f32[1,256,256]{2,1,0:T(8,128)}, u32[]{:S(2)}) copy-start(f32[1,256,256]{2,1,0:T(8,128)} %param.16) | copy-start | bytes 786436
  12.4 0.7 copy-start.5
  12.4 0.7 copy-start.4
  12.4 1.0 copy-start.3
  12.4 4.0 copy-start.6
  12.4 7.7 %copy-start = (f32[1,2560,256]{2,1,0:T(8,128)S(1)}, f32[1,2560,256]{2,1,0:T(8,128)}, u32[]{:S(2)}) copy-start(f32[1,2560,256]{2,1,0:T(8,128)} %param.15) | copy-start | bytes 7864324
  426.7 3.5 copy-start.2
Sparse Core Ops, SparseCore 0:
  12.6 72.8 all-gather.1
where the time goes:
time: 444 us; the launch traced here: 438 us
  Pallas kernels  346 us (78%)
  waiting for transfers between devices  63.5 us (14%)
  between operations  14.8 us (3%)
  other arithmetic  7.44 us (2%)
  local copies, waits for them, and re-layouts  5.58 us (1%)
    pallas_call x1, Pallas kernels, reduce_rows(): pl.pallas_call(functools.partial(reduce_kernel, line, flat_first, chunks)...  137 us
    pallas_call x1, Pallas kernels, product(): pl.pallas_call(functools.partial(product_kernel, siblings, tile_blocks, c...  107 us
    pallas_call x1, Pallas kernels, finish(): pl.pallas_call(functools.partial(finish_kernel, row_count, col_count), ou...  92.8 us
    all_gather x1, waiting for transfers between devices, per_device(): panels = lax.all_gather(flipped(l_store[0]), 'col', tiled=True)  63.5 us
  transfers between devices with their start and end apart: 1, of which 1 were waited for; matrix products, arithmetic and copies ran while one was open for 2% of the time, Pallas kernels for 0%

commit v1 on v0

--- a/solution.py
+++ b/solution.py
@@ -8,6 +8,7 @@
 from jax.sharding import PartitionSpec as P
 
 BLK = 128
+GROUP = 4
 MESH = pl.DeviceIdType.MESH
 
 
@@ -18,27 +19,32 @@
     return jnp.any(entry_hits, axis=1)
 
 
-def product_kernel(siblings, tile_blocks, col_blocks, row_blocks,
-                   slot_ref, rows_ref, count_ref, column_ref,
-                   a_ref, panels_ref, out_ref, a_high, a_low, p_high, p_low, acc):
-    stripe = pl.program_id(0)
-    width = out_ref.shape[0]
+def product_kernel(members, tile_blocks, col_blocks, row_blocks, joins,
+                   slot_ref, rows_ref, count_ref, a_ref, *refs):
+    panel_refs, refs = refs[:members], refs[members + joins:]
+    out_ref, a_high, a_low, p_high, p_low, stage, sent = refs
+    stripe, stripes = pl.program_id(0), pl.num_programs(0)
+    group = p_high.shape[3] // BLK
+    listed = p_high.shape[1] * group
 
     @pl.when(stripe == 0)
     def _():
-        for sibling in range(siblings):
-            column = column_ref[sibling]
-
-            @pl.loop(0, row_blocks)
-            def _(block):
-                lanes = pl.ds(pl.multiple_of(block * BLK, BLK), BLK)
-                value = panels_ref[pl.ds(pl.multiple_of(column * width, width), width), lanes]
+        for member in range(members):
+            @pl.loop(0, count_ref[member])
+            def _(i):
+                rows = pl.ds(pl.multiple_of(rows_ref[member * listed + i] * BLK, BLK), BLK)
+                lanes = pl.ds(pl.multiple_of(lax.rem(i, group) * BLK, BLK), BLK)
+                value = -panel_refs[member][rows, :].T
                 high = value.astype(jnp.bfloat16)
-                p_high[sibling, block] = high
-                p_low[sibling, block] = (value - high.astype(jnp.float32)).astype(jnp.bfloat16)
-
-            p_high[sibling, row_blocks] = jnp.zeros(p_high.shape[2:], jnp.bfloat16)
-            p_low[sibling, row_blocks] = jnp.zeros(p_low.shape[2:], jnp.bfloat16)
+                p_high[member, i // group, :, lanes] = high
+                p_low[member, i // group, :, lanes] = (value - high.astype(jnp.float32)).astype(jnp.bfloat16)
+
+            @pl.loop(count_ref[member], (count_ref[member] + group - 1) // group * group)
+            def _(i):
+                lanes = pl.ds(pl.multiple_of(lax.rem(i, group) * BLK, BLK), BLK)
+                zero = jnp.zeros((p_high.shape[2], BLK), jnp.bfloat16)
+                p_high[member, i // group, :, lanes] = zero
+                p_low[member, i // group, :, lanes] = zero
 
     @pl.loop(0, row_blocks)
     def _(block):
@@ -48,78 +54,92 @@
         a_high[block] = high
         a_low[block] = (value - high.astype(jnp.float32)).astype(jnp.bfloat16)
 
-    for sibling in range(siblings):
-        acc[...] = jnp.zeros_like(acc)
-        base = sibling * (row_blocks + 1)
-
-        @pl.loop(0, (count_ref[sibling] + 1) // 2)
-        def _(pair):
-            first = rows_ref[base + 2 * pair]
-            second = rows_ref[base + 2 * pair + 1]
-            second_a = jnp.minimum(second, row_blocks - 1)
-            ph = [p_high[sibling, first], p_high[sibling, second]]
-            plo = [p_low[sibling, first], p_low[sibling, second]]
-            ah = [a_high[first], a_high[second_a]]
-            al = [a_low[first], a_low[second_a]]
-            left = jnp.concatenate(ph + ph + plo, axis=1)
-            right = jnp.concatenate(ah + al + ah, axis=0)
-            acc[...] += jnp.dot(left, right, preferred_element_type=jnp.float32)
-
+    def slot_of(member, block, at):
+        return slot_ref[member * col_blocks + at * tile_blocks + block]
+
+    def slot_copy(member, block, slot):
+        return pltpu.make_async_copy(
+            stage.at[member, :, pl.ds(block * BLK, BLK)],
+            out_ref.at[:, pl.ds(pl.multiple_of(slot * BLK, BLK), BLK)],
+            sent.at[member, block],
+        )
+
+    def settle(member, at):
         for block in range(tile_blocks):
-            slot = slot_ref[sibling * col_blocks + stripe * tile_blocks + block]
+            slot = slot_of(member, block, at)
 
             @pl.when(slot >= 0)
             def _():
-                out_ref[:, pl.ds(pl.multiple_of(slot * BLK, BLK), BLK)] = (
-                    -acc[:, block * BLK:(block + 1) * BLK]
-                )
-
-
-def product(slot, rows, counts, columns, anc, panels, width, cap):
-    siblings = counts.shape[0]
+                slot_copy(member, block, slot).wait()
+
+    for member in range(members):
+        @pl.when(stripe > 0)
+        def _():
+            settle(member, stripe - 1)
+
+        stage[member] = jnp.zeros(stage.shape[1:], jnp.float32)
+
+        @pl.loop(0, (count_ref[member] + group - 1) // group)
+        def _(k):
+            at = [rows_ref[member * listed + k * group + u] for u in range(group)]
+            ph, plo = p_high[member, k], p_low[member, k]
+            ah, al = [a_high[i] for i in at], [a_low[i] for i in at]
+            left = jnp.concatenate([ph, ph, plo], axis=1)
+            right = jnp.concatenate(ah + al + ah, axis=0)
+            stage[member] += jnp.dot(left, right, preferred_element_type=jnp.float32)
+
+        for block in range(tile_blocks):
+            slot = slot_of(member, block, stripe)
+
+            @pl.when(slot >= 0)
+            def _():
+                slot_copy(member, block, slot).start()
+
+    @pl.when(stripe == stripes - 1)
+    def _():
+        for member in range(members):
+            settle(member, stripe)
+
+
+def product(slot, rows, counts, anc, panels, slots_all, partial_value=None):
+    members = counts.shape[0]
     depth, cells = anc.shape
+    width = panels[0].shape[1]
     row_blocks, col_blocks = depth // BLK, cells // BLK
-    tile_blocks = next(n for n in (4, 2, 1) if col_blocks % n == 0)
+    tile_blocks = next(n for n in (8, 4, 2, 1) if col_blocks % n == 0)
     tile = tile_blocks * BLK
+    groups = rows.shape[1] // GROUP
+    joins = () if partial_value is None else (partial_value,)
+    held = pl.BlockSpec((depth, width), lambda i, *_: (0, 0), pipeline_mode=pl.Buffered(1))
     return pl.pallas_call(
-        functools.partial(product_kernel, siblings, tile_blocks, col_blocks, row_blocks),
-        out_shape=jax.ShapeDtypeStruct((width, cap * BLK), jnp.float32),
+        functools.partial(product_kernel, members, tile_blocks, col_blocks, row_blocks, len(joins)),
+        out_shape=jax.ShapeDtypeStruct((width, slots_all * BLK), jnp.float32),
         grid_spec=pltpu.PrefetchScalarGridSpec(
-            num_scalar_prefetch=4,
+            num_scalar_prefetch=3,
             grid=(col_blocks // tile_blocks,),
-            in_specs=[
-                pl.BlockSpec((depth, tile), lambda i, *_: (0, i)),
-                pl.BlockSpec(panels.shape, lambda i, *_: (0, 0), pipeline_mode=pl.Buffered(1)),
-            ],
-            out_specs=pl.BlockSpec((width, cap * BLK), lambda i, *_: (0, 0), pipeline_mode=pl.Buffered(1)),
+            in_specs=[pl.BlockSpec((depth, tile), lambda i, *_: (0, i))]
+            + [held] * members
+            + [pl.BlockSpec(memory_space=pl.ANY)] * len(joins),
+            out_specs=pl.BlockSpec(memory_space=pl.ANY),
             scratch_shapes=[
                 pltpu.VMEM((row_blocks, BLK, tile), jnp.bfloat16),
                 pltpu.VMEM((row_blocks, BLK, tile), jnp.bfloat16),
-                pltpu.VMEM((siblings, row_blocks + 1, width, BLK), jnp.bfloat16),
-                pltpu.VMEM((siblings, row_blocks + 1, width, BLK), jnp.bfloat16),
-                pltpu.VMEM((width, tile), jnp.float32),
+                pltpu.VMEM((members, groups, width, GROUP * BLK), jnp.bfloat16),
+                pltpu.VMEM((members, groups, width, GROUP * BLK), jnp.bfloat16),
+                pltpu.VMEM((members, width, tile), jnp.float32),
+                pltpu.SemaphoreType.DMA((members, tile_blocks)),
             ],
+        ),
+        input_output_aliases={4 + members: 0} if joins else {},
+        cost_estimate=pl.CostEstimate(
+            flops=2 * 3 * members * depth * cells * width // 2,
+            bytes_accessed=4 * depth * cells + 4 * members * width * cells,
+            transcendentals=0,
         ),
         compiler_params=pltpu.CompilerParams(
             dimension_semantics=("arbitrary",), vmem_limit_bytes=63 * 1024 * 1000
         ),
-    )(slot, rows, counts, columns, anc, panels)
-
-
-def flip_kernel(value_ref, out_ref):
-    out_ref[...] = value_ref[...].T
-
-
-def flipped(value):
-    depth, width = value.shape
-    step = next(n for n in (512, 256, 128) if depth % n == 0)
-    return pl.pallas_call(
-        flip_kernel,
-        out_shape=jax.ShapeDtypeStruct((width, depth), value.dtype),
-        grid=(depth // step,),
-        in_specs=[pl.BlockSpec((step, width), lambda i: (i, 0))],
-        out_specs=pl.BlockSpec((width, step), lambda i: (0, i)),
-    )(value)
+    )(slot.reshape(-1), rows.reshape(-1), counts, anc, *panels, *joins)
 
 
 def expand_kernel(siblings, col_count, col_blocks, slot_ref, owner_ref, compact_ref, upper_ref, slots_ref):
@@ -154,8 +174,8 @@
 
 def reduce_kernel(line, flat_first, chunks,
                   partial_ref, out_ref,
-                  pair_buf, up_buf, down_buf, flat_up, flat_down, flat_sum, flat_pair,
-                  pair_send, pair_recv, up_send, up_recv, down_send, down_recv, flat_send, flat_recv):
+                  mine, flat_mine, pair_buf, up_buf, down_buf, flat_up, flat_down, flat_sum, flat_pair,
+                  mine_sem, flat_sem, pair_send, pair_recv, up_send, up_recv, down_send, down_recv, flat_send, flat_recv):
     r, c = lax.axis_index("row"), lax.axis_index("col")
     z, y = r // 2, lax.rem(r, 2)
     other = 1 - y
@@ -166,6 +186,18 @@
     def lanes(chunk):
         return pl.ds(pl.multiple_of(chunk * width, width), width)
 
+    def flat_load(k):
+        return pltpu.make_async_copy(partial_ref.at[:, :, :, lanes(k)], flat_mine.at[k], flat_sem.at[k])
+
+    def pair_load(k):
+        return pltpu.make_async_copy(
+            partial_ref.at[:, y, :, lanes(k + flat_first)], mine.at[k], mine_sem.at[k]
+        )
+
+    @pl.loop(0, flat_first)
+    def _(k):
+        flat_load(k).start()
+
     barrier = pltpu.get_barrier_semaphore()
     pl.semaphore_signal(barrier, inc=1, device_id=(z * 2 + other, c), device_id_type=MESH)
 
@@ -221,7 +253,7 @@
 
     def flat(k):
         def own(place):
-            return partial_ref[place, :, :, lanes(k)]
+            return flat_mine[k, place]
 
         def finish(value):
             flat_sum[k] = value
@@ -286,15 +318,21 @@
     @pl.loop(0, late)
     def _(k):
         pair_copy(k).start()
+        pair_load(k).start()
 
     @pl.loop(0, chunks + lag * last)
     def _(i):
+        @pl.when(i < flat_first)
+        def _():
+            flat_load(i).wait()
+
         @pl.when((i >= flat_first) & (i < chunks))
         def _():
             k = i - flat_first
+            pair_load(k).wait()
             pair_copy(k).wait_recv()
             for place in range(line):
-                pair_buf[k, place] = pair_buf[k, place] + partial_ref[place, y, :, lanes(i)]
+                pair_buf[k, place] = pair_buf[k, place] + mine[k, place]
 
         for at in range(line):
             @pl.when(z == at)
@@ -330,20 +368,21 @@
                         down_copy(buf, k, k + shift, at).wait_send()
 
 
-def reduce_rows(value, row_count, chunks, collective):
+def reduce_rows(value, row_count, chunks, lanes, collective):
     width, columns = value.shape
     line, slice_rows = row_count // 2, width // row_count
-    lanes = columns // chunks
     flat_first = (chunks + 3) // 6
     late = chunks - flat_first
     vmem = pl.BlockSpec(memory_space=pltpu.VMEM)
     dma = pltpu.SemaphoreType.DMA
     return pl.pallas_call(
         functools.partial(reduce_kernel, line, flat_first, chunks),
-        out_shape=jax.ShapeDtypeStruct((slice_rows, columns), jnp.float32),
-        in_specs=[vmem],
+        out_shape=jax.ShapeDtypeStruct((slice_rows, chunks * lanes), jnp.float32),
+        in_specs=[pl.BlockSpec(memory_space=pl.ANY)],
         out_specs=vmem,
         scratch_shapes=[
+            pltpu.VMEM((late, line, slice_rows, lanes), jnp.float32),
+            pltpu.VMEM((flat_first, line, 2, slice_rows, lanes), jnp.float32),
             pltpu.VMEM((late, line, slice_rows, lanes), jnp.float32),
             pltpu.VMEM((late, line - 1, slice_rows, lanes), jnp.float32),
             pltpu.VMEM((late, line - 1, slice_rows, lanes), jnp.float32),
@@ -351,6 +390,8 @@
             pltpu.VMEM((flat_first, line - 1, 2, slice_rows, lanes), jnp.float32),
             pltpu.VMEM((flat_first, 2, slice_rows, lanes), jnp.float32),
             pltpu.VMEM((flat_first, slice_rows, lanes), jnp.float32),
+            dma((late,)),
+            dma((flat_first,)),
             dma((late,)),
             dma((late,)),
             dma((chunks,)),
@@ -598,7 +639,14 @@
     row_count, col_count = lax.axis_size("row"), lax.axis_size("col")
     r, c = lax.axis_index("row"), lax.axis_index("col")
     row_blocks, col_blocks = anc_inverse.shape[0] // BLK, anc_inverse.shape[1] // BLK
-    panels = lax.all_gather(flipped(l_store[0]), "col", tiled=True)
+    pairs = col_count // 2
+    mate = [(k, k + 1 - 2 * (k % 2)) for k in range(col_count)]
+    panel = l_store[0]
+    near = [panel, lax.ppermute(panel, "col", mate)]
+    moved = [
+        lax.ppermute(panel, "col", [(k, (k + 2 * step) % col_count) for k in range(col_count)])
+        for step in range(1, pairs)
+    ]
 
     table = listed_table(block_lists, block_counts, row_blocks * row_count)
     row_listed = lax.dynamic_slice_in_dim(table, r * row_blocks, row_blocks, axis=1)
@@ -607,17 +655,16 @@
     counts = jnp.sum(row_ints, axis=1)
     place = jnp.cumsum(row_ints, axis=1) - 1
     ids = jnp.arange(row_blocks, dtype=jnp.int32)
-    entry = jnp.arange(row_blocks + 1, dtype=jnp.int32)
+    entry = jnp.arange(-(-row_blocks // GROUP) * GROUP, dtype=jnp.int32)
     hits = row_listed[:, :, None] & (place[:, :, None] == entry[None, None, :])
-    rows = jnp.sum(jnp.where(hits, ids[None, :, None], 0), axis=1)
-    rows = jnp.where(entry[None, :] < counts[:, None], rows, row_blocks).astype(jnp.int32).reshape(-1)
+    rows = jnp.sum(jnp.where(hits, ids[None, :, None], 0), axis=1).astype(jnp.int32)
 
     flat = col_listed.reshape(-1)
     slot = jnp.where(flat, jnp.cumsum(flat.astype(jnp.int32)) - 1, -1).astype(jnp.int32)
     per_column = jnp.sum(table.reshape(siblings, col_count, col_blocks).astype(jnp.int32), axis=(0, 2))
     needed = jnp.max(per_column)
-    slots_all = siblings * col_blocks
-    grain = -(-slots_all // 40)
+    slots_all = -(-siblings * col_blocks // 40) * 40
+    grain = slots_all // 40
     caps = [grain * n for n in (19, 21, 23, 25, 28, 32, 40)]
     level = jnp.sum((needed > jnp.array(caps[:-1], jnp.int32)).astype(jnp.int32))
 
@@ -630,14 +677,40 @@
     own = l_store[0] * jnp.repeat(own_listed.astype(jnp.float32), BLK)[:, None]
     base = jnp.sum(mine.astype(jnp.float32)) * diag_inv[0]
 
+    slot_rows = slot.reshape(siblings, col_blocks)
+
+    def pick(column):
+        sibling = lax.dynamic_index_in_dim(owner, column, keepdims=False)
+        at = jnp.maximum(sibling, 0)
+        there = sibling >= 0
+        return (
+            jnp.where(there, slot_rows[at], -1),
+            rows[at],
+            jnp.where(there, counts[at], 0),
+        )
+
+    def tables(columns):
+        found = [pick(column) for column in columns]
+        return [jnp.stack(part) for part in zip(*found)]
+
+    mate_of = c + 1 - 2 * (c % 2)
+    near_columns = [c, mate_of]
+    far_columns = []
+    for step in range(1, pairs):
+        far_columns += [lax.rem(c - 2 * step + col_count, col_count), lax.rem(mate_of - 2 * step + col_count, col_count)]
+    partial_value = product(*tables(near_columns), anc_inverse, near, slots_all)
+    if moved:
+        moved, partial_value = lax.optimization_barrier((moved, partial_value))
+        far = [panel for one in moved for panel in (one, lax.ppermute(one, "col", mate))]
+        partial_value = product(*tables(far_columns), anc_inverse, far, slots_all, partial_value)
+
     def branch(place, cap):
-        def run(anc, panels):
-            partial_value = product(slot, rows, counts, sibling_columns, anc, panels, l_store.shape[2], cap)
-            compact = reduce_rows(partial_value, row_count, cap // grain, place + 1)
+        def run(value):
+            compact = reduce_rows(value, row_count, cap // grain, grain * BLK, place + 1)
             return expand(slot, owner, compact, siblings, col_blocks)
         return run
 
-    upper, slots = lax.switch(level, [branch(place, cap) for place, cap in enumerate(caps)], anc_inverse, panels)
+    upper, slots = lax.switch(level, [branch(place, cap) for place, cap in enumerate(caps)], partial_value)
     lower, diag = finish(slots, own, base, row_count)
     return upper, lower[None], diag[None]
 

time: 444 us -> 371 us (0.84)
  waiting for transfers between devices: 63.5 us -> 0.01 us
  Pallas kernels: 346 us -> 331 us
  other arithmetic: 7.44 us -> 13.2 us
  between operations: 14.8 us -> 9.21 us
    all_gather x1 -> x0, waiting for transfers between devices: 63.5 us -> none  [per_device(): panels = lax.all_gather(flipped(l_store[0]), 'col', tiled=True)]
    pallas_call x2, Pallas kernels: 112 us -> 79.3 us  [product(): pl.pallas_call(functools.partial(product_kernel, members, tile_blocks, co...]
    pallas_call x1, Pallas kernels: 137 us -> 154 us  [reduce_rows(): pl.pallas_call(functools.partial(reduce_kernel, line, flat_first, chunks)...]
  transfers between devices with their start and end apart: 1 -> 3, of which waited for: 1 -> 0; matrix products, arithmetic and copies ran while one was open for 2% -> 5% of each run, Pallas kernels for 0% -> 12%
where the time goes in v1:
time: 371 us; the launch traced here: 366 us
  Pallas kernels  331 us (89%)
  other arithmetic  13.2 us (4%)
  between operations  9.21 us (2%)
  local copies, waits for them, and re-layouts  8.8 us (2%)
  starting transfers between devices  3.73 us (1%)
    pallas_call x1, Pallas kernels, reduce_rows(): pl.pallas_call(functools.partial(reduce_kernel, line, flat_first, chunks)...  154 us
    pallas_call x1, Pallas kernels, finish(): pl.pallas_call(functools.partial(finish_kernel, row_count, col_count), ou...  93.7 us
    pallas_call x2, Pallas kernels, product(): pl.pallas_call(functools.partial(product_kernel, members, tile_blocks, co...  79.3 us
  transfers between devices with their start and end apart: 3, of which 0 were waited for; matrix products, arithmetic and copies ran while one was open for 5% of the time, Pallas kernels for 12%

profile of v1, /device:TPU:0, one launch (start us, length us, event | category | flops | bytes accessed | tf_op | source)
XLA Modules:
  0.0 365.7 jit_solution(2425614360553015818)
XLA Ops:
  0.6 3.0 collective-permute-start
  3.7 0.7 iota_compare_fusion.3
  4.4 0.7 select_reduce_fusion.1
  5.2 0.7 fusion.6
  11.1 0.9 fusion.1
  12.9 1.3 convert_reduce_fusion.2
  14.9 0.6 reshape.119.slot_ref
  15.6 0.7 reshape.120.rows_ref
  16.4 0.7 fusion.5
  18.9 44.9 %shard_map.94.refs_2_ = f32[256,20480]{1,0:T(8,128)} custom-call(s32[80]{0:T(128)} %reshape.119.slot_ref, s32[40]{0:T(128)} %reshape.120.rows_ref, s32[2]{0:T(128)} %pad_add_fusion.5.count_ref, f32[2560,5120]{1,0:T(8,128)} %a_ref.3, f32[2560,256]{1,0:T(8,128)} %bitcast.44, f32[2560,256]{1,0:T(8,128)} %collective-permute-done.1.refs_1_), custom_call_target="tpu_custom_call" | custom-call | flops 20132659200 | bytes 62914560 | tf_op jit(solution)/shard_map/pallas_call | solution.py:114
  63.8 0.7 collective-permute-start.2
  65.4 0.6 reshape.118.rows_ref
  67.3 0.6 reduce_max.18
  67.9 1.3 fusion.4
  69.8 0.7 pad_add_fusion.4.count_ref
  70.6 1.4 multiply_bitcast_fusion.base_ref
  72.0 3.6 broadcast_multiply_fusion.own_ref
  75.6 34.4 %shard_map.95 = f32[256,20480]{1,0:T(8,128)} custom-call(s32[80]{0:T(128)} %reshape.117.slot_ref, s32[40]{0:T(128)} %reshape.118.rows_ref, s32[2]{0:T(128)} %pad_add_fusion.4.count_ref, f32[2560,5120]{1,0:T(8,128)} %a_ref.3, f32[2560,256]{1,0:T(8,128)} %collective-permute-done.refs_0_, ...), custom_call_target="tpu_custom_call", output_to_operand_aliasing={{}: (6, {})} | custom-call | flops 20132659200 | bytes 62914560 | tf_op jit(solution)/shard_map/pallas_call | solution.py:114
  110.0 157.8 %conditional.1 = ((f32[4,32,5120]{2,1,0:T(8,128)}, f32[4,32,5120]{2,1,0:T(8,128)S(1)})) conditional(s32[]{:T(128)} %clamp.3, (f32[256,20480]{1,0:T(8,128)}, s32[160]{0:T(256)S(1)}, s32[4]{0:T(128)S(1)}) %tuple.31, (f32[256,20480]{1,0:T(8,128)}, s32[160]{0:T(256)S(1)}, s32[4]{0:T(128)S(1)}) %tuple.31, ...), branch_computations={%region_11.12_spmd, %region_12.13_spmd, %region_13.14_spmd, %regio... | conditional | bytes 8 | solution.py:713
  110.1 153.8 %branch_2_fun.2.compact_ref = f32[32,11776]{1,0:T(8,128)} custom-call(f32[4,2,32,20480]{3,2,1,0:T(8,128)} %bitcast.37), custom_call_target="tpu_custom_call" | custom-call | tf_op jit(solution)/shard_map/cond/branch_2_fun/pallas_call | solution.py:378
  263.9 3.9 %branch_2_fun.3 = (f32[4,32,5120]{2,1,0:T(8,128)}, f32[4,32,5120]{2,1,0:T(8,128)S(1)}) custom-call(s32[160]{0:T(256)S(1)} %get-tuple-element.48.slot_ref, s32[4]{0:T(128)S(1)} %get-tuple-element.49.owner_ref, f32[32,11776]{1,0:T(8,128)} %branch_2_fun.2.compact_ref), custom_call_target="tpu_custom_call" | custom-call | tf_op jit(solution)/shard_map/cond/branch_2_fun/pallas_call | solution.py:164
  267.8 93.7 %shard_map.96 = (f32[2560,256]{1,0:T(8,128)}, f32[256,256]{1,0:T(8,128)}) custom-call(f32[4,32,5120]{2,1,0:T(8,128)S(1)} %get-tuple-element.75.slots_ref, f32[2560,256]{1,0:T(8,128)} %broadcast_multiply_fusion.own_ref, f32[256,256]{1,0:T(8,128)} %multiply_bitcast_fusion.base_ref), custom_call_target="tpu_custom_call" | custom-call | tf_op jit(solution)/shard_map/pallas_call | solution.py:609
  361.6 3.4 copy.30
  365.0 0.7 copy.31
  (42 shorter events, 3.3 us)
Async XLA Ops:
  0.6 63.2 %collective-permute-start = (f32[2560,256]{1,0:T(8,128)}, f32[2560,256]{1,0:T(8,128)}, u32[]{:S(2)}, u32[]{:S(2)}) collective-permute-start(f32[2560,256]{1,0:T(8,128)} %bitcast.42), channel_id=1, source_target_pairs={{0,2},{1,3},{2,0},{3,1},{4,6},{5,7},{6,4},{7,5},{8,10},{9,11},{10,... | collective-permute-start | bytes 7864328 | tf_op jit(solution)/shard_map/ppermute | solution.py:647
  3.7 15.3 %collective-permute-start.1 = (f32[2560,256]{1,0:T(8,128)}, f32[2560,256]{1,0:T(8,128)}, u32[]{:S(2)}, u32[]{:S(2)}) collective-permute-start(f32[2560,256]{1,0:T(8,128)} %bitcast.43), channel_id=1, source_target_pairs={{0,1},{1,0},{2,3},{3,2},{4,5},{5,4},{6,7},{7,6},{8,9},{9,8},{10,11... | collective-permute-start | bytes 7864328 | tf_op jit(solution)/shard_map/ppermute | solution.py:645
  18.9 49.0 %copy-start.2 = (s32[6]{0:T(128)S(1)}, s32[6]{0:T(128)}, u32[]{:S(2)}) copy-start(s32[6]{0:T(128)} %constant.87.clone) | copy-start | bytes 76
  18.9 51.6 %copy-start = (f32[1,256,256]{2,1,0:T(8,128)S(1)}, f32[1,256,256]{2,1,0:T(8,128)}, u32[]{:S(2)}) copy-start(f32[1,256,256]{2,1,0:T(8,128)} %param.16) | copy-start | bytes 786436
  63.8 11.8 %collective-permute-start.2 = (f32[2560,256]{1,0:T(8,128)}, f32[2560,256]{1,0:T(8,128)}, u32[]{:S(2)}, u32[]{:S(2)}) collective-permute-start(f32[2560,256]{1,0:T(8,128)} %collective-permute-done.refs_0_), channel_id=1, source_target_pairs={{0,1},{1,0},{2,3},{3,2},{4,5},{5,4},{6,7},{7,6},{8,9},{9,8},{10,11... | collective-permute-start | bytes 7864328 | tf_op jit(solution)/shard_map/ppermute | solution.py:704
  361.5 3.5 copy-start.1
